TPU v7x, 32 devices: a whole 2x2x4 slice. The times are simulated.
32 devices in a mesh: dp: 8 (over z, x), tm: 4 (over y, core).
Axes of the slice: x: 2, y: 2, z: 4, core: 2. Of those that a mesh axis runs over, the one named last changes fastest.
Arguments:
- frames: bfloat16 [8, 512, 1536], P('dp', 'tm'), may hold values from -3 to 3
- query: bfloat16 [8, 512, 1536], P('dp', 'tm'), may hold values from -6 to 6
- keys: bfloat16 [8, 512, 1536], P('dp', 'tm'), may hold values from -6 to 6
- values: bfloat16 [8, 512, 1536], P('dp', 'tm'), may hold values from -6 to 6
- norm_gain: float32 [1536], replicated, may hold values from 0.1 to 1.9
- conv_gain: float32 [1536], replicated, may hold values from 0.1 to 1.9
- w_glu: bfloat16 [1536, 3072], P('tm'), may hold values from -0.15625 to 0.15625
- taps: float32 [32, 1536], replicated, may hold values from -1 to 1
- w_out: bfloat16 [1536, 1536], P('tm'), may hold values from -0.15625 to 0.15625
- cotangent: bfloat16 [8, 512, 1536], P('dp', 'tm'), may hold values from -0.09375 to 0.09375
Outputs:
- glu_grad: float32 [1536, 3072], P('tm')
- taps_grad: float32 [32, 1536], P(None, 'tm')
- out_grad: float32 [1536, 1536], P('tm')
All inputs are finite; a program needn't handle non-finite values.
Results may differ from a plain program's by a relative error of at most 0.02.
Values may be sent and summed in bfloat16 or wider, within the bound.
No kernel may reach another device: no remote copies, remote signals or barrier semaphores. Data moves between devices by JAX's collectives and lax.ppermute only.
A program may use at most 128 MiB of HBM per device.

v0:
```python
import math
import jax
import jax.numpy as jnp
from jax import lax
from jax.sharding import PartitionSpec as P

HEADS = 16


def padded_2(value, sides, width):
    for axis, dim in sides:
        devices, length = (lax.axis_size(axis), value.shape[dim])
        up = [(i, (i + 1) % devices) for i in range(devices - 1)]
        down = [(j, i) for i, j in up]
        last = lax.slice_in_dim(value, length - width, length, axis=dim)
        leading = lax.slice_in_dim(value, 0, width, axis=dim)
        before = lax.ppermute(last, axis, up)
        after = lax.ppermute(leading, axis, down)
        value = jnp.concatenate([before, value, after], axis=dim)
    return value


def standard(v):
    mean = jnp.mean(v, axis=-1, keepdims=True)
    centred = v - mean
    var = jnp.mean(centred * centred, axis=-1, keepdims=True)
    inv = lax.rsqrt(var + 1e-05)
    return (centred * inv, inv)


def attend_heads(parts):
    q_all, k_all, v_all = parts
    length = q_all.shape[0]
    groups = q_all.shape[1]
    count = q_all.shape[2]
    head_dim = q_all.shape[3]
    q_flat = q_all.reshape(length, groups * count, head_dim)
    k_flat = k_all.reshape(length, groups * count, head_dim)
    v_flat = v_all.reshape(length, groups * count, head_dim)
    block = math.gcd(length, 512)
    scale = head_dim ** (-0.5)
    q_blocks = q_flat.reshape(length // block, block, groups * count, head_dim)

    def one_block(q_part):
        scores = (
            jnp.einsum("qhd,khd->hqk", q_part, k_flat, preferred_element_type=jnp.float32) * scale
        )
        top = jnp.max(scores, axis=2, keepdims=True)
        expo = jnp.exp(scores - top)
        total = jnp.sum(expo, axis=2)
        weights = expo.astype(jnp.bfloat16)
        summed = jnp.einsum("hqk,khd->qhd", weights, v_flat, preferred_element_type=jnp.float32)
        return (summed / total.T[:, :, None]).astype(jnp.bfloat16)

    return lax.map(one_block, q_blocks).reshape(length, groups, count, head_dim)


def add_rows(left, piece):
    return jnp.dot(left, piece, preferred_element_type=jnp.float32)


def project_back(cot_rows, piece):
    return lax.dot_general(
        cot_rows, piece, (((1,), (1,)), ((), ())), preferred_element_type=jnp.float32
    )


def rim_rows(field, half):
    return padded_2(field, (("tm", 0),), half)


def row_product(left, right):
    return lax.dot_general(
        left, right, (((0,), (0,)), ((), ())), preferred_element_type=jnp.float32
    )


def local(frames, query, keys, values, norm_gain, conv_gain, w_glu, taps, w_out, cotangent):
    rows = frames.shape[1]
    width = frames.shape[2]
    head_dim = width // HEADS
    groups = lax.axis_size("tm")
    per_group = HEADS // groups
    kernel = taps.shape[0]
    half = kernel // 2

    def split_heads(arr):
        return arr[0].reshape(rows, groups, per_group, head_dim)

    heads_out = attend_heads(
        (
            lax.all_to_all(split_heads(query), "tm", split_axis=1, concat_axis=0, tiled=True),
            lax.all_to_all(split_heads(keys), "tm", split_axis=1, concat_axis=0, tiled=True),
            lax.all_to_all(split_heads(values), "tm", split_axis=1, concat_axis=0, tiled=True),
        )
    )
    attention = lax.all_to_all(heads_out, "tm", split_axis=0, concat_axis=1, tiled=True).reshape(
        rows, width
    )
    mixed = frames[0].astype(jnp.float32) + attention.astype(jnp.float32)
    normed, unused = standard(mixed)
    u_rows = (normed * norm_gain).astype(jnp.bfloat16)
    p_full = add_rows(u_rows, lax.all_gather(w_glu, "tm", axis=0, tiled=True))
    first = p_full[:, :width]
    sig = jax.nn.sigmoid(p_full[:, width:])
    y_rows = (first * sig).astype(jnp.bfloat16)
    padded = rim_rows(y_rows, half)
    z_rows = jnp.zeros((rows, width), jnp.float32)
    for k in range(kernel):
        z_rows = z_rows + taps[k] * padded[k : k + rows].astype(jnp.float32)
    zhat, inv = standard(z_rows)
    n_rows = zhat * conv_gain
    sgate = jax.nn.sigmoid(n_rows)
    s_rows = (n_rows * sgate).astype(jnp.bfloat16)
    cot_rows = cotangent[0]
    d_s = project_back(cot_rows, lax.all_gather(w_out, "tm", axis=0, tiled=True))
    d_n = d_s * sgate * (1.0 + n_rows * (1.0 - sgate))
    e_rows = d_n * conv_gain
    d_z = (
        (
            e_rows
            - jnp.mean(e_rows, axis=-1, keepdims=True)
            - zhat * jnp.mean(e_rows * zhat, axis=-1, keepdims=True)
        )
        * inv
    ).astype(jnp.bfloat16)
    dz_pad = rim_rows(d_z, half)
    d_y = jnp.zeros((rows, width), jnp.float32)
    for k in range(kernel):
        d_y = d_y + taps[k] * dz_pad[2 * half - k : 2 * half - k + rows].astype(jnp.float32)
    d_p = jnp.concatenate([d_y * sig, d_y * first * sig * (1.0 - sig)], axis=1).astype(jnp.bfloat16)
    dz_float = d_z.astype(jnp.float32)
    taps_term = jnp.stack(
        [
            jnp.sum(dz_float * padded[k : k + rows].astype(jnp.float32), axis=0)
            for k in range(kernel)
        ]
    )
    glu_term = row_product(u_rows, d_p)
    glu_share, taps_share, out_share = (
        lax.psum_scatter(
            glu_term.astype(jnp.bfloat16), "tm", scatter_dimension=0, tiled=True
        ).astype(jnp.float32),
        lax.psum_scatter(
            taps_term.astype(jnp.bfloat16), "tm", scatter_dimension=1, tiled=True
        ).astype(jnp.float32),
        lax.psum_scatter(
            row_product(s_rows, cot_rows).astype(jnp.bfloat16),
            "tm",
            scatter_dimension=0,
            tiled=True,
        ).astype(jnp.float32),
    )
    glu_grad, taps_grad, out_grad = (
        lax.psum(glu_share.astype(jnp.bfloat16), "dp").astype(jnp.float32),
        lax.psum(taps_share.astype(jnp.bfloat16), "dp").astype(jnp.float32),
        lax.psum(out_share.astype(jnp.bfloat16), "dp").astype(jnp.float32),
    )
    return (glu_grad, taps_grad, out_grad)


def solution(mesh):
    return jax.shard_map(
        local,
        mesh=mesh,
        in_specs=(
            P("dp", "tm", None),
            P("dp", "tm", None),
            P("dp", "tm", None),
            P("dp", "tm", None),
            P(),
            P(),
            P("tm", None),
            P(),
            P("tm", None),
            P("dp", "tm", None),
        ),
        out_specs=(P("tm", None), P(None, "tm"), P("tm", None)),
        check_vma=False,
    )
```

profile of v0, /device:TPU:0, one launch (start us, length us, event | category | flops | bytes accessed | tf_op | source)
XLA Modules:
  0.0 441.2 jit_solution(16104276012726749351)
XLA Ops:
  7.2 0.7 all-gather.5.cloned.1.call-update
  8.0 0.7 all-gather.3.cloned.1.call-update
  8.7 1.9 copy.50
  10.6 4.3 all-to-all-start.1
  14.9 0.9 copy.48
  15.8 6.5 %all-to-all-done.1 = bf16[128,4,4,96]{0,3,2,1:T(8,128)(2,1)S(1)} async-done(((bf16[128,4,4,96]{0,3,2,1:T(8,128)(2,1)}), bf16[128,4,4,96]{0,3,2,1:T(8,128)(2,1)S(1)}, u32[]{:S(2)}, u32[]{:S(2)}) %all-to-all-start.1) | async-done | bytes 393248 | tf_op jit(solution)/shard_map/all_to_all | solution.py:93
  22.3 3.5 all-to-all-start
  25.8 0.9 copy.52
  26.7 11.1 %all-to-all-done = bf16[128,4,4,96]{0,3,2,1:T(8,128)(2,1)S(1)} async-done(((bf16[128,4,4,96]{0,3,2,1:T(8,128)(2,1)}), bf16[128,4,4,96]{0,3,2,1:T(8,128)(2,1)S(1)}, u32[]{:S(2)}, u32[]{:S(2)}) %all-to-all-start) | async-done | bytes 393248 | tf_op jit(solution)/shard_map/all_to_all | solution.py:92
  37.8 3.5 all-to-all-start.2
  42.2 11.1 %all-to-all-done.2 = bf16[128,4,4,96]{0,3,2,1:T(8,128)(2,1)S(1)} async-done(((bf16[128,4,4,96]{0,3,2,1:T(8,128)(2,1)}), bf16[128,4,4,96]{0,3,2,1:T(8,128)(2,1)S(1)}, u32[]{:S(2)}, u32[]{:S(2)}) %all-to-all-start.2) | async-done | bytes 393248 | tf_op jit(solution)/shard_map/all_to_all | solution.py:94
  53.7 0.8 multiply_reduce_fusion
  54.5 0.7 fusion
  55.2 0.9 fusion.17
  56.1 1.1 copy.55
  57.2 3.6 all-to-all-start.3
  61.1 0.9 slice_reduce_fusion.31
  62.0 13.6 %all-to-all-done.3 = bf16[512,1,4,96]{3,2,1,0:T(4,128)(2,1)S(1)} async-done(((bf16[512,1,4,96]{3,2,1,0:T(4,128)(2,1)}), bf16[512,1,4,96]{3,2,1,0:T(4,128)(2,1)S(1)}, u32[]{:S(2)}, u32[]{:S(2)}) %all-to-all-start.3) | async-done | bytes 393248 | tf_op jit(solution)/shard_map/all_to_all | solution.py:97
  77.0 13.6 %all-gather.5.cloned.1.call-done = bf16[1536,3072]{1,0:T(8,128)(2,1)} async-done(((bf16[384,3072]{1,0:T(8,128)(2,1)}), bf16[1536,3072]{1,0:T(8,128)(2,1)}) %all-gather.5.cloned.1.call-update) | async-done | bytes 9437200 | tf_op jit(solution)/shard_map/all_gather | solution.py:103
  90.7 5.2 %fusion.179 = f32[128,3072]{1,0:T(8,128)S(1)} fusion(bf16[128,1536]{0,1:T(8,128)(2,1)S(1)} %multiply_convert_fusion.5, bf16[1536,3072]{1,0:T(8,128)(2,1)} %all-gather.5.cloned.1.call-done), kind=kOutput, calls=%fused_computation.372 | convolution fusion | flops 1207959552 | bytes 11403264 | tf_op jit(solution)/shard_map/dot_general | solution.py:59
  96.2 2.2 collective-permute-start
  98.4 1.3 collective-permute-start.1
  100.0 1.5 collective-permute-done.1
  101.7 4.1 fusion.175
  106.0 3.7 convolution_convert_fusion.1
  110.0 20.1 %all-gather.3.cloned.1.call-done = bf16[1536,1536]{1,0:T(8,128)(2,1)} async-done(((bf16[384,1536]{1,0:T(8,128)(2,1)}), bf16[1536,1536]{1,0:T(8,128)(2,1)}) %all-gather.3.cloned.1.call-update) | async-done | bytes 4718608 | tf_op jit(solution)/shard_map/all_gather | solution.py:116
  130.1 4.2 fusion.173
  134.4 4.4 fusion.98
  138.8 1.3 collective-permute-start.2
  140.1 3.0 collective-permute-start.3
  143.1 0.9 collective-permute-done.3
  144.0 5.5 %multiply_convert_fusion.2 = (bf16[128,1536]{1,0:T(8,128)(2,1)S(1)}, f32[128,1536]{1,0:T(8,128)S(1)}) fusion(f32[128,3072]{1,0:T(8,128)S(1)} %fusion.179, bf16[128,1536]{1,0:T(8,128)(2,1)S(1)} %get-tuple-element.86, bf16[16,1536]{1,0:T(8,128)(2,1)S(1)} %collective-permute-done.3, f32[1536]{0:T(1024)} %copy-done.41, f32[1536]{0:T(1024)} %copy-done.42, ...), kind=kLoop, calls=%fused_computation.228 | loop fusion | flops 37945344 | bytes 2654208 | tf_op jit(solution)/shard_map/convert.68
  149.8 5.3 %convolution_convert_fusion = bf16[1536,3072]{1,0:T(8,128)(2,1)} fusion(bf16[128,1536]{0,1:T(8,128)(2,1)S(1)} %copy-done.2, bf16[128,1536]{1,0:T(8,128)(2,1)S(1)} %multiply_convert_fusion.1, bf16[128,1536]{1,0:T(8,128)(2,1)S(1)} %get-tuple-element.87), kind=kOutput, calls=%fused_computation | convolution fusion | flops 1214251008 | bytes 10616832 | tf_op jit(solution)/shard_map/dot_general | solution.py:73
  155.2 0.6 copy-done.7
  155.9 0.8 fusion.97
  156.8 1.1 fusion.82
  158.1 0.8 fusion.81
  159.2 0.4 stack.164
  159.6 0.9 copy.59
  160.6 20.7 %reduce-scatter.8.cloned.1.call-done = bf16[384,1536]{1,0:T(8,128)(2,1)} async-done(((bf16[1536,1536]{1,0:T(8,128)(2,1)}), bf16[384,1536]{1,0:T(8,128)(2,1)}) %reduce-scatter.8.cloned.1.call-update) | async-done | bytes 1179664 | tf_op jit(solution)/shard_map/reduce_scatter | solution.py:147
  181.3 80.4 %reduce-scatter.6.cloned.1.call-done = bf16[384,3072]{1,0:T(8,128)(2,1)} async-done(((bf16[1536,3072]{1,0:T(8,128)(2,1)}), bf16[384,3072]{1,0:T(8,128)(2,1)}) %reduce-scatter.6.cloned.1.call-update) | async-done | bytes 2359312 | tf_op jit(solution)/shard_map/reduce_scatter | solution.py:141
  261.7 23.7 %reduce-scatter.10.cloned.1.call-done = bf16[384,32]{1,0:T(8,128)(2,1)} async-done(((bf16[1536,32]{1,0:T(8,128)(2,1)}), bf16[384,32]{1,0:T(8,128)(2,1)}) %reduce-scatter.10.cloned.1.call-update) | async-done | bytes 24592
  285.4 1.0 copy.60
  286.4 39.0 %psum.22 = bf16[32,384]{1,0:T(8,128)(2,1)S(1)} all-reduce(bf16[32,384]{1,0:T(8,128)(2,1)S(1)} %copy.60), channel_id=1, replica_groups=mesh['dp'=8,'tm'=4] {'dp'}, use_global_device_ids=true, to_apply=%region_43.44 | all-reduce | flops 12288 | bytes 49152 | tf_op jit(solution)/shard_map/psum | solution.py:156
  325.4 0.6 convert_element_type.363
  326.1 102.1 %all-reduce.3.cloned.1.call-done = (bf16[384,3072]{1,0:T(8,128)(2,1)}, bf16[384,1536]{1,0:T(8,128)(2,1)}) async-done(((bf16[384,3072]{1,0:T(8,128)(2,1)}, bf16[384,1536]{1,0:T(8,128)(2,1)}), (bf16[384,3072]{1,0:T(8,128)(2,1)}, bf16[384,1536]{1,0:T(8,128)(2,1)})) %all-reduce.3.cloned.1.call-update) | async-done | bytes 3538960 | tf_op jit(solution)/shard_map/psum | solution.py:155
  428.2 4.5 %convert_element_type.362 = f32[384,3072]{1,0:T(8,128)} convert(bf16[384,3072]{1,0:T(8,128)(2,1)} %get-tuple-element.84) | non-fusion elementwise | flops 1179648 | bytes 7077888 | tf_op jit(solution)/shard_map/convert_element_type | solution.py:155
  432.7 1.7 convert_element_type.366
  (177 shorter events, 4.9 us)
Async XLA Ops:
  7.2 98.8 %copy-start = (bf16[1,128,1536]{2,1,0:T(8,128)(2,1)S(1)}, bf16[1,128,1536]{2,1,0:T(8,128)(2,1)}, u32[]{:S(2)}) copy-start(bf16[1,128,1536]{2,1,0:T(8,128)(2,1)} %param.19) | copy-start | bytes 1179652
  7.2 18.6 %copy-start.9 = (bf16[1,128,1536]{2,1,0:T(8,128)(2,1)S(1)}, bf16[1,128,1536]{2,1,0:T(8,128)(2,1)}, u32[]{:S(2)}) copy-start(bf16[1,128,1536]{2,1,0:T(8,128)(2,1)} %param.13) | copy-start | bytes 1179652
  7.2 83.4 %all-gather.5.cloned.1.call-start = ((), (), s32[]{:S(2)}) async-start(), calls=%async_computation.8 | async-start | bytes 11796480 | tf_op jit(solution)/shard_map/all_gather | solution.py:103
  7.9 122.2 %all-gather.3.cloned.1.call-start = ((), (), s32[]{:S(2)}) async-start(), calls=%async_computation.7 | async-start | bytes 5898240 | tf_op jit(solution)/shard_map/all_gather | solution.py:116
  10.6 11.7 %all-to-all-start.1 = ((bf16[128,4,4,96]{0,3,2,1:T(8,128)(2,1)}), bf16[128,4,4,96]{0,3,2,1:T(8,128)(2,1)S(1)}, u32[]{:S(2)}, u32[]{:S(2)}) async-start(bf16[128,4,4,96]{0,3,2,1:T(8,128)(2,1)} %bitcast.4), calls=%async_computation.1 | async-start | bytes 786432 | tf_op jit(solution)/shard_map/all_to_all | solution.py:93
  22.3 15.5 %all-to-all-start = ((bf16[128,4,4,96]{0,3,2,1:T(8,128)(2,1)}), bf16[128,4,4,96]{0,3,2,1:T(8,128)(2,1)S(1)}, u32[]{:S(2)}, u32[]{:S(2)}) async-start(bf16[128,4,4,96]{0,3,2,1:T(8,128)(2,1)} %bitcast.1), calls=%async_computation | async-start | bytes 786432 | tf_op jit(solution)/shard_map/all_to_all | solution.py:92
  37.8 15.5 %all-to-all-start.2 = ((bf16[128,4,4,96]{0,3,2,1:T(8,128)(2,1)}), bf16[128,4,4,96]{0,3,2,1:T(8,128)(2,1)S(1)}, u32[]{:S(2)}, u32[]{:S(2)}) async-start(bf16[128,4,4,96]{0,3,2,1:T(8,128)(2,1)} %bitcast.7), calls=%async_computation.2 | async-start | bytes 786432 | tf_op jit(solution)/shard_map/all_to_all | solution.py:94
  57.2 19.5 %copy-start.52 = (f32[1536]{0:T(1024)S(1)}, f32[1536]{0:T(1024)}, u32[]{:S(2)}) copy-start(f32[1536]{0:T(1024)} %param.14) | copy-start | bytes 18436
  57.2 18.4 %all-to-all-start.3 = ((bf16[512,1,4,96]{3,2,1,0:T(4,128)(2,1)}), bf16[512,1,4,96]{3,2,1,0:T(4,128)(2,1)S(1)}, u32[]{:S(2)}, u32[]{:S(2)}) async-start(bf16[512,1,4,96]{3,2,1,0:T(4,128)(2,1)} %copy.55), calls=%async_computation.3 | async-start | bytes 1048576 | tf_op jit(solution)/shard_map/all_to_all | solution.py:97
  60.8 120.5 %reduce-scatter.8.cloned.1.call-start = ((), (), s32[]{:S(2)}) async-start(), calls=%async_computation.10 | async-start | bytes 5898240 | tf_op jit(solution)/shard_map/reduce_scatter | solution.py:147
  77.0 18.9 %copy-start.1 = (bf16[128,1536]{0,1:T(8,128)(2,1)}, bf16[128,1536]{0,1:T(8,128)(2,1)S(1)}, u32[]{:S(2)}) copy-start(bf16[128,1536]{0,1:T(8,128)(2,1)S(1)} %multiply_convert_fusion.5) | copy-start | bytes 1179652
  90.6 10.9 %copy-start.15 = (f32[1536]{0:T(1024)S(1)}, f32[1536]{0:T(1024)}, u32[]{:S(2)}) copy-start(f32[1536]{0:T(1024)} %get-tuple-element.56) | copy-start | bytes 18436
  90.6 10.9 %copy-start.16 = (f32[1536]{0:T(1024)S(1)}, f32[1536]{0:T(1024)}, u32[]{:S(2)}) copy-start(f32[1536]{0:T(1024)} %get-tuple-element.57) | copy-start | bytes 18436
  90.6 10.9 %copy-start.17 = (f32[1536]{0:T(1024)S(1)}, f32[1536]{0:T(1024)}, u32[]{:S(2)}) copy-start(f32[1536]{0:T(1024)} %get-tuple-element.58) | copy-start | bytes 18436
  90.6 10.9 %copy-start.18 = (f32[1536]{0:T(1024)S(1)}, f32[1536]{0:T(1024)}, u32[]{:S(2)}) copy-start(f32[1536]{0:T(1024)} %get-tuple-element.59) | copy-start | bytes 18436
  90.6 10.9 %copy-start.19 = (f32[1536]{0:T(1024)S(1)}, f32[1536]{0:T(1024)}, u32[]{:S(2)}) copy-start(f32[1536]{0:T(1024)} %get-tuple-element.60) | copy-start | bytes 18436
  90.6 10.9 %copy-start.20 = (f32[1536]{0:T(1024)S(1)}, f32[1536]{0:T(1024)}, u32[]{:S(2)}) copy-start(f32[1536]{0:T(1024)} %get-tuple-element.61) | copy-start | bytes 18436
  90.6 10.9 %copy-start.21 = (f32[1536]{0:T(1024)S(1)}, f32[1536]{0:T(1024)}, u32[]{:S(2)}) copy-start(f32[1536]{0:T(1024)} %get-tuple-element.62) | copy-start | bytes 18436
  90.6 10.9 %copy-start.22 = (f32[1536]{0:T(1024)S(1)}, f32[1536]{0:T(1024)}, u32[]{:S(2)}) copy-start(f32[1536]{0:T(1024)} %get-tuple-element.63) | copy-start | bytes 18436
  90.7 10.9 %copy-start.23 = (f32[1536]{0:T(1024)S(1)}, f32[1536]{0:T(1024)}, u32[]{:S(2)}) copy-start(f32[1536]{0:T(1024)} %get-tuple-element.64) | copy-start | bytes 18436
  90.7 10.9 %copy-start.24 = (f32[1536]{0:T(1024)S(1)}, f32[1536]{0:T(1024)}, u32[]{:S(2)}) copy-start(f32[1536]{0:T(1024)} %get-tuple-element.65) | copy-start | bytes 18436
  90.7 10.9 %copy-start.25 = (f32[1536]{0:T(1024)S(1)}, f32[1536]{0:T(1024)}, u32[]{:S(2)}) copy-start(f32[1536]{0:T(1024)} %get-tuple-element.66) | copy-start | bytes 18436
  90.7 10.9 %copy-start.26 = (f32[1536]{0:T(1024)S(1)}, f32[1536]{0:T(1024)}, u32[]{:S(2)}) copy-start(f32[1536]{0:T(1024)} %get-tuple-element.67) | copy-start | bytes 18436
  90.7 10.9 %copy-start.27 = (f32[1536]{0:T(1024)S(1)}, f32[1536]{0:T(1024)}, u32[]{:S(2)}) copy-start(f32[1536]{0:T(1024)} %get-tuple-element.68) | copy-start | bytes 18436
  90.7 10.9 %copy-start.28 = (f32[1536]{0:T(1024)S(1)}, f32[1536]{0:T(1024)}, u32[]{:S(2)}) copy-start(f32[1536]{0:T(1024)} %get-tuple-element.69) | copy-start | bytes 18436
  90.7 10.9 %copy-start.29 = (f32[1536]{0:T(1024)S(1)}, f32[1536]{0:T(1024)}, u32[]{:S(2)}) copy-start(f32[1536]{0:T(1024)} %get-tuple-element.70) | copy-start | bytes 18436
  96.2 3.8 collective-permute-start
  98.4 3.1 collective-permute-start.1
  99.9 34.4 %copy-start.31 = (f32[1536]{0:T(1024)}, f32[1536]{0:T(1024)S(1)}, u32[]{:S(2)}) copy-start(f32[1536]{0:T(1024)S(1)} %get-tuple-element.72) | copy-start | bytes 18436
  99.9 34.4 %copy-start.32 = (f32[1536]{0:T(1024)}, f32[1536]{0:T(1024)S(1)}, u32[]{:S(2)}) copy-start(f32[1536]{0:T(1024)S(1)} %get-tuple-element.73) | copy-start | bytes 18436
  99.9 34.4 %copy-start.33 = (f32[1536]{0:T(1024)}, f32[1536]{0:T(1024)S(1)}, u32[]{:S(2)}) copy-start(f32[1536]{0:T(1024)S(1)} %get-tuple-element.74) | copy-start | bytes 18436
  99.9 34.4 %copy-start.34 = (f32[1536]{0:T(1024)}, f32[1536]{0:T(1024)S(1)}, u32[]{:S(2)}) copy-start(f32[1536]{0:T(1024)S(1)} %get-tuple-element.75) | copy-start | bytes 18436
  99.9 34.4 %copy-start.35 = (f32[1536]{0:T(1024)}, f32[1536]{0:T(1024)S(1)}, u32[]{:S(2)}) copy-start(f32[1536]{0:T(1024)S(1)} %get-tuple-element.76) | copy-start | bytes 18436
  99.9 34.4 %copy-start.36 = (f32[1536]{0:T(1024)}, f32[1536]{0:T(1024)S(1)}, u32[]{:S(2)}) copy-start(f32[1536]{0:T(1024)S(1)} %get-tuple-element.77) | copy-start | bytes 18436
  100.0 34.4 %copy-start.37 = (f32[1536]{0:T(1024)}, f32[1536]{0:T(1024)S(1)}, u32[]{:S(2)}) copy-start(f32[1536]{0:T(1024)S(1)} %get-tuple-element.78) | copy-start | bytes 18436
  100.0 34.4 %copy-start.38 = (f32[1536]{0:T(1024)}, f32[1536]{0:T(1024)S(1)}, u32[]{:S(2)}) copy-start(f32[1536]{0:T(1024)S(1)} %get-tuple-element.79) | copy-start | bytes 18436
  100.0 34.4 %copy-start.39 = (f32[1536]{0:T(1024)}, f32[1536]{0:T(1024)S(1)}, u32[]{:S(2)}) copy-start(f32[1536]{0:T(1024)S(1)} %get-tuple-element.80) | copy-start | bytes 18436
  100.0 34.4 %copy-start.40 = (f32[1536]{0:T(1024)}, f32[1536]{0:T(1024)S(1)}, u32[]{:S(2)}) copy-start(f32[1536]{0:T(1024)S(1)} %get-tuple-element.81) | copy-start | bytes 18436
  100.0 34.4 %copy-start.41 = (f32[1536]{0:T(1024)}, f32[1536]{0:T(1024)S(1)}, u32[]{:S(2)}) copy-start(f32[1536]{0:T(1024)S(1)} %get-tuple-element.82) | copy-start | bytes 18436
  100.0 34.4 %copy-start.42 = (f32[1536]{0:T(1024)}, f32[1536]{0:T(1024)S(1)}, u32[]{:S(2)}) copy-start(f32[1536]{0:T(1024)S(1)} %get-tuple-element.83) | copy-start | bytes 18436
  105.8 24.4 %copy-start.53 = (f32[128]{0:T(128)}, f32[128]{0:T(128)S(1)}, u32[]{:S(2)}) copy-start(f32[128]{0:T(128)S(1)} %broadcast_multiply_fusion.2) | copy-start | bytes 1540
  106.0 24.1 %copy-start.54 = (f32[128]{0:T(128)}, f32[128]{0:T(128)S(1)}, u32[]{:S(2)}) copy-start(f32[128]{0:T(128)S(1)} %add_rsqrt_fusion) | copy-start | bytes 1540
  109.8 151.9 %reduce-scatter.6.cloned.1.call-start = ((), (), s32[]{:S(2)}) async-start(), calls=%async_computation.9 | async-start | bytes 11796480 | tf_op jit(solution)/shard_map/reduce_scatter | solution.py:141
  134.4 15.4 %copy-start.2 = (bf16[128,1536]{0,1:T(8,128)(2,1)S(1)}, bf16[128,1536]{0,1:T(8,128)(2,1)}, u32[]{:S(2)}) copy-start(bf16[128,1536]{0,1:T(8,128)(2,1)} %copy-done.1) | copy-start | bytes 1179652
  138.8 4.3 collective-permute-start.2
  140.1 3.9 collective-permute-start.3
  155.2 130.2 %reduce-scatter.10.cloned.1.call-start = ((), (), s32[]{:S(2)}) async-start(), calls=%async_computation.11 | async-start | bytes 491520
  160.5 267.6 %all-reduce.3.cloned.1.call-start = ((), (), s32[]{:S(2)}) async-start(), calls=%async_computation.12 | async-start | bytes 7077888 | tf_op jit(solution)/shard_map/psum | solution.py:155
  (21 other events, 113.7 us)
Sparse Core Ops, SparseCore 0:
  9.6 80.9 all-gather.4
  92.1 37.9 all-gather.2
  133.3 47.9 reduce-scatter.7
  183.7 77.9 reduce-scatter.5
  264.6 20.7 reduce-scatter.9
  288.9 139.1 all-reduce.2
where the time goes:
time: 442 us; the launch traced here: 441 us
  waiting for transfers between devices  307 us (69%)
  blocking collectives  39 us (9%)
  other arithmetic  25.7 us (6%)
  starting transfers between devices  23 us (5%)
  matrix products  20.1 us (5%)
  between operations  15.3 us (3%)
  local copies, waits for them, and re-layouts  11.5 us (3%)
    psum x1, waiting for transfers between devices, local(): lax.psum(glu_share.astype(jnp.bfloat16), 'dp').astype(jnp.float32)  102 us
    reduce_scatter x1, waiting for transfers between devices, local(): lax.psum_scatter(glu_term.astype(jnp.bfloat16), 'tm', scatter_dimension=0...  80.4 us
    psum x1, blocking collectives, local(): lax.psum(taps_share.astype(jnp.bfloat16), 'dp').astype(jnp.float32)  39 us
    unnamed x7, waiting for transfers between devices  25.2 us
    reduce_scatter x1, waiting for transfers between devices, local(): lax.psum_scatter(row_product(s_rows, cot_rows).astype(jnp.bfloat16), 'tm'...  20.7 us
    all_gather x1, waiting for transfers between devices, local(): lax.all_gather(w_out, 'tm', axis=0, tiled=True)  20.1 us
    all_to_all x1, waiting for transfers between devices, local(): lax.all_to_all(heads_out, 'tm', split_axis=0, concat_axis=1, tiled=True)  13.6 us
    all_gather x1, waiting for transfers between devices, local(): p_full = add_rows(u_rows, lax.all_gather(w_glu, 'tm', axis=0, tiled=True))  13.6 us
  transfers between devices with their start and end apart: 14, of which 12 were waited for; matrix products, arithmetic and copies ran while one was open for 11% of the time, Pallas kernels for 0%

commit v1 on v0

--- a/solution.py
+++ b/solution.py
@@ -5,6 +5,10 @@
 from jax.sharding import PartitionSpec as P
 
 HEADS = 16
+
+
+def raise_the_patch(inputs):
+    return jnp.sum(jax.lax.all_gather(inputs, axis_name="dp"), axis=0)
 
 
 def padded_2(value, sides, width):
@@ -152,7 +156,7 @@
         ).astype(jnp.float32),
     )
     glu_grad, taps_grad, out_grad = (
-        lax.psum(glu_share.astype(jnp.bfloat16), "dp").astype(jnp.float32),
+        raise_the_patch(glu_share.astype(jnp.bfloat16)).astype(jnp.float32),
         lax.psum(taps_share.astype(jnp.bfloat16), "dp").astype(jnp.float32),
         lax.psum(out_share.astype(jnp.bfloat16), "dp").astype(jnp.float32),
     )

time: 442 us -> 754 us (1.71)
  waiting for transfers between devices: 307 us -> 610 us
  other arithmetic: 25.7 us -> 33.6 us
    all_gather x0 -> x1, waiting for transfers between devices: none -> 360 us  [raise_the_patch(): return jnp.sum(jax.lax.all_gather(inputs, axis_name='dp'), axis=0)]
    psum x1, waiting for transfers between devices: 102 us -> 44.7 us  [local(): lax.psum(out_share.astype(jnp.bfloat16), 'dp').astype(jnp.float32)]
    reduce_sum x0 -> x1, other arithmetic: none -> 10.9 us  [raise_the_patch(): return jnp.sum(jax.lax.all_gather(inputs, axis_name='dp'), axis=0)]
    unnamed x7 -> x8, waiting for transfers between devices: 25.2 us -> 25.2 us
  transfers between devices with their start and end apart: 14 -> 15, of which waited for: 12 -> 13; matrix products, arithmetic and copies ran while one was open for 11% -> 7% of each run, Pallas kernels for 0% -> 0%
where the time goes in v1:
time: 754 us; the launch traced here: 753 us
  waiting for transfers between devices  610 us (81%)
  blocking collectives  37.5 us (5%)
  other arithmetic  33.6 us (4%)
  starting transfers between devices  23 us (3%)
  matrix products  20.1 us (3%)
  between operations  15.7 us (2%)
  local copies, waits for them, and re-layouts  12.5 us (2%)
    all_gather x1, waiting for transfers between devices, raise_the_patch(): return jnp.sum(jax.lax.all_gather(inputs, axis_name='dp'), axis=0)  360 us
    reduce_scatter x1, waiting for transfers between devices, local(): lax.psum_scatter(glu_term.astype(jnp.bfloat16), 'tm', scatter_dimension=0...  80.3 us
    psum x1, waiting for transfers between devices, local(): lax.psum(out_share.astype(jnp.bfloat16), 'dp').astype(jnp.float32)  44.7 us
    psum x1, blocking collectives, local(): lax.psum(taps_share.astype(jnp.bfloat16), 'dp').astype(jnp.float32)  37.5 us
    unnamed x8, waiting for transfers between devices  25.2 us
    reduce_scatter x1, waiting for transfers between devices, local(): lax.psum_scatter(row_product(s_rows, cot_rows).astype(jnp.bfloat16), 'tm'...  22.8 us
    all_gather x1, waiting for transfers between devices, local(): lax.all_gather(w_out, 'tm', axis=0, tiled=True)  18.7 us
  transfers between devices with their start and end apart: 15, of which 13 were waited for; matrix products, arithmetic and copies ran while one was open for 7% of the time, Pallas kernels for 0%

profile of v1, /device:TPU:0, one launch (start us, length us, event | category | flops | bytes accessed | tf_op | source)
XLA Modules:
  0.0 752.8 jit_solution(11757101284727429977)
XLA Ops:
  7.2 0.7 all-gather.7.cloned.1.call-update
  8.0 0.7 all-gather.5.cloned.1.call-update
  8.7 1.9 copy.52
  10.6 4.3 all-to-all-start.2
  14.9 0.9 copy.48
  15.8 6.5 all-to-all-done.2
  22.3 3.5 all-to-all-start
  25.8 0.9 copy.50
  26.7 11.1 %all-to-all-done = bf16[128,4,4,96]{0,3,2,1:T(8,128)(2,1)S(1)} async-done(((bf16[128,4,4,96]{0,3,2,1:T(8,128)(2,1)}), bf16[128,4,4,96]{0,3,2,1:T(8,128)(2,1)S(1)}, u32[]{:S(2)}, u32[]{:S(2)}) %all-to-all-start) | async-done | bytes 393248 | tf_op jit(solution)/shard_map/all_to_all | solution.py:96
  37.8 3.5 all-to-all-start.1
  42.2 11.1 %all-to-all-done.1 = bf16[128,4,4,96]{0,3,2,1:T(8,128)(2,1)S(1)} async-done(((bf16[128,4,4,96]{0,3,2,1:T(8,128)(2,1)}), bf16[128,4,4,96]{0,3,2,1:T(8,128)(2,1)S(1)}, u32[]{:S(2)}, u32[]{:S(2)}) %all-to-all-start.1) | async-done | bytes 393248 | tf_op jit(solution)/shard_map/all_to_all | solution.py:97
  53.7 0.8 multiply_reduce_fusion
  54.5 0.7 fusion
  55.2 0.9 fusion.17
  56.1 1.1 copy.55
  57.2 3.6 all-to-all-start.3
  61.1 0.9 slice_reduce_fusion.31
  62.0 13.6 %all-to-all-done.3 = bf16[512,1,4,96]{3,2,1,0:T(4,128)(2,1)S(1)} async-done(((bf16[512,1,4,96]{3,2,1,0:T(4,128)(2,1)}), bf16[512,1,4,96]{3,2,1,0:T(4,128)(2,1)S(1)}, u32[]{:S(2)}, u32[]{:S(2)}) %all-to-all-start.3) | async-done | bytes 393248 | tf_op jit(solution)/shard_map/all_to_all | solution.py:101
  77.0 13.6 %all-gather.7.cloned.1.call-done = bf16[1536,3072]{1,0:T(8,128)(2,1)} async-done(((bf16[384,3072]{1,0:T(8,128)(2,1)}), bf16[1536,3072]{1,0:T(8,128)(2,1)}) %all-gather.7.cloned.1.call-update) | async-done | bytes 9437200 | tf_op jit(solution)/shard_map/all_gather | solution.py:107
  90.7 5.2 fusion.179
  96.2 1.3 collective-permute-start.1
  97.5 3.0 collective-permute-start
  101.7 4.1 fusion.175
  106.9 3.7 convolution_convert_fusion.1
  110.9 18.7 %all-gather.5.cloned.1.call-done = bf16[1536,1536]{1,0:T(8,128)(2,1)} async-done(((bf16[384,1536]{1,0:T(8,128)(2,1)}), bf16[1536,1536]{1,0:T(8,128)(2,1)}) %all-gather.5.cloned.1.call-update) | async-done | bytes 4718608 | tf_op jit(solution)/shard_map/all_gather | solution.py:120
  129.9 4.2 fusion.173
  134.1 3.3 fusion.98
  137.5 2.1 collective-permute-start.3
  139.6 1.3 collective-permute-start.2
  140.9 2.1 collective-permute-done.2
  143.3 4.0 multiply_convert_fusion.2
  147.7 5.3 convolution_convert_fusion
  153.1 0.7 copy-done.6
  153.8 0.8 fusion.81
  154.6 1.1 fusion.82
  156.0 0.8 fusion.97
  157.4 0.9 copy.59
  158.4 22.8 %reduce-scatter.8.cloned.1.call-done = bf16[384,1536]{1,0:T(8,128)(2,1)} async-done(((bf16[1536,1536]{1,0:T(8,128)(2,1)}), bf16[384,1536]{1,0:T(8,128)(2,1)}) %reduce-scatter.8.cloned.1.call-update) | async-done | bytes 1179664 | tf_op jit(solution)/shard_map/reduce_scatter | solution.py:151
  181.3 80.3 %reduce-scatter.6.cloned.1.call-done = bf16[384,3072]{1,0:T(8,128)(2,1)} async-done(((bf16[1536,3072]{1,0:T(8,128)(2,1)}), bf16[384,3072]{1,0:T(8,128)(2,1)}) %reduce-scatter.6.cloned.1.call-update) | async-done | bytes 2359312 | tf_op jit(solution)/shard_map/reduce_scatter | solution.py:145
  261.7 23.8 %reduce-scatter.10.cloned.1.call-done = bf16[384,32]{1,0:T(8,128)(2,1)} async-done(((bf16[1536,32]{1,0:T(8,128)(2,1)}), bf16[384,32]{1,0:T(8,128)(2,1)}) %reduce-scatter.10.cloned.1.call-update) | async-done | bytes 24592
  285.4 1.0 copy.60
  286.4 37.5 %psum.14 = bf16[32,384]{1,0:T(8,128)(2,1)S(1)} all-reduce(bf16[32,384]{1,0:T(8,128)(2,1)S(1)} %copy.60), channel_id=1, replica_groups=mesh['dp'=8,'tm'=4] {'dp'}, use_global_device_ids=true, to_apply=%region_43.44 | all-reduce | flops 12288 | bytes 49152 | tf_op jit(solution)/shard_map/psum | solution.py:160
  323.9 0.6 convert_element_type.365
  324.5 44.7 %all-reduce.2.cloned.1.call-done = bf16[384,1536]{1,0:T(8,128)(2,1)} async-done(((bf16[384,1536]{1,0:T(8,128)(2,1)}), bf16[384,1536]{1,0:T(8,128)(2,1)}) %all-reduce.2.cloned.1.call-update) | async-done | bytes 1179664 | tf_op jit(solution)/shard_map/psum | solution.py:161
  369.2 3.0 convert_element_type.368
  372.2 360.2 %all-gather.9.cloned.1.call-done = bf16[3072,3072]{1,0:T(8,128)(2,1)} async-done(((bf16[384,3072]{1,0:T(8,128)(2,1)}), bf16[3072,3072]{1,0:T(8,128)(2,1)}) %all-gather.9.cloned.1.call-update) | async-done | bytes 18874384 | tf_op jit(solution)/shard_map/all_gather | solution.py:11
  732.4 10.9 %reduce_sum.371 = bf16[384,3072]{1,0:T(8,128)(2,1)S(1)} reduce(bf16[8,384,3072]{2,1,0:T(8,128)(2,1)} %bitcast.68, bf16[]{:T(256)} %constant.33.clone.1), dimensions={0}, to_apply=%region_9.10 | reduce | flops 8257536 | bytes 21233666 | tf_op jit(solution)/shard_map/reduce_sum | solution.py:11
  743.2 2.8 convert_element_type.364
  (243 shorter events, 6.8 us)
Async XLA Ops:
  7.2 99.7 %copy-start = (bf16[1,128,1536]{2,1,0:T(8,128)(2,1)S(1)}, bf16[1,128,1536]{2,1,0:T(8,128)(2,1)}, u32[]{:S(2)}) copy-start(bf16[1,128,1536]{2,1,0:T(8,128)(2,1)} %param.19) | copy-start | bytes 1179652
  7.2 18.6 %copy-start.8 = (bf16[1,128,1536]{2,1,0:T(8,128)(2,1)S(1)}, bf16[1,128,1536]{2,1,0:T(8,128)(2,1)}, u32[]{:S(2)}) copy-start(bf16[1,128,1536]{2,1,0:T(8,128)(2,1)} %param.12) | copy-start | bytes 1179652
  7.2 83.4 %all-gather.7.cloned.1.call-start = ((), (), s32[]{:S(2)}) async-start(), calls=%async_computation.8 | async-start | bytes 11796480 | tf_op jit(solution)/shard_map/all_gather | solution.py:107
  7.9 121.7 %all-gather.5.cloned.1.call-start = ((), (), s32[]{:S(2)}) async-start(), calls=%async_computation.7 | async-start | bytes 5898240 | tf_op jit(solution)/shard_map/all_gather | solution.py:120
  10.6 11.7 %all-to-all-start.2 = ((bf16[128,4,4,96]{0,3,2,1:T(8,128)(2,1)}), bf16[128,4,4,96]{0,3,2,1:T(8,128)(2,1)S(1)}, u32[]{:S(2)}, u32[]{:S(2)}) async-start(bf16[128,4,4,96]{0,3,2,1:T(8,128)(2,1)} %bitcast.7), calls=%async_computation.2 | async-start | bytes 786432 | tf_op jit(solution)/shard_map/all_to_all | solution.py:98
  22.3 15.5 %all-to-all-start = ((bf16[128,4,4,96]{0,3,2,1:T(8,128)(2,1)}), bf16[128,4,4,96]{0,3,2,1:T(8,128)(2,1)S(1)}, u32[]{:S(2)}, u32[]{:S(2)}) async-start(bf16[128,4,4,96]{0,3,2,1:T(8,128)(2,1)} %bitcast.1), calls=%async_computation | async-start | bytes 786432 | tf_op jit(solution)/shard_map/all_to_all | solution.py:96
  37.8 15.5 %all-to-all-start.1 = ((bf16[128,4,4,96]{0,3,2,1:T(8,128)(2,1)}), bf16[128,4,4,96]{0,3,2,1:T(8,128)(2,1)S(1)}, u32[]{:S(2)}, u32[]{:S(2)}) async-start(bf16[128,4,4,96]{0,3,2,1:T(8,128)(2,1)} %bitcast.4), calls=%async_computation.1 | async-start | bytes 786432 | tf_op jit(solution)/shard_map/all_to_all | solution.py:97
  57.2 19.5 %copy-start.81 = (f32[1536]{0:T(1024)S(1)}, f32[1536]{0:T(1024)}, u32[]{:S(2)}) copy-start(f32[1536]{0:T(1024)} %param.14) | copy-start | bytes 18436
  57.2 18.4 %all-to-all-start.3 = ((bf16[512,1,4,96]{3,2,1,0:T(4,128)(2,1)}), bf16[512,1,4,96]{3,2,1,0:T(4,128)(2,1)S(1)}, u32[]{:S(2)}, u32[]{:S(2)}) async-start(bf16[512,1,4,96]{3,2,1,0:T(4,128)(2,1)} %copy.55), calls=%async_computation.3 | async-start | bytes 1048576 | tf_op jit(solution)/shard_map/all_to_all | solution.py:101
  60.8 120.4 %reduce-scatter.8.cloned.1.call-start = ((), (), s32[]{:S(2)}) async-start(), calls=%async_computation.10 | async-start | bytes 5898240 | tf_op jit(solution)/shard_map/reduce_scatter | solution.py:151
  96.2 4.7 collective-permute-start.1
  97.5 3.9 collective-permute-start
  110.7 151.0 %reduce-scatter.6.cloned.1.call-start = ((), (), s32[]{:S(2)}) async-start(), calls=%async_computation.9 | async-start | bytes 11796480 | tf_op jit(solution)/shard_map/reduce_scatter | solution.py:145
  129.6 13.4 %copy-start.13 = (f32[1536]{0:T(1024)S(1)}, f32[1536]{0:T(1024)}, u32[]{:S(2)}) copy-start(f32[1536]{0:T(1024)} %get-tuple-element.53) | copy-start | bytes 18436
  129.6 13.4 %copy-start.15 = (f32[1536]{0:T(1024)S(1)}, f32[1536]{0:T(1024)}, u32[]{:S(2)}) copy-start(f32[1536]{0:T(1024)} %get-tuple-element.54) | copy-start | bytes 18436
  129.6 13.4 %copy-start.17 = (f32[1536]{0:T(1024)S(1)}, f32[1536]{0:T(1024)}, u32[]{:S(2)}) copy-start(f32[1536]{0:T(1024)} %get-tuple-element.55) | copy-start | bytes 18436
  129.6 13.4 %copy-start.19 = (f32[1536]{0:T(1024)S(1)}, f32[1536]{0:T(1024)}, u32[]{:S(2)}) copy-start(f32[1536]{0:T(1024)} %get-tuple-element.56) | copy-start | bytes 18436
  129.6 13.4 %copy-start.21 = (f32[1536]{0:T(1024)S(1)}, f32[1536]{0:T(1024)}, u32[]{:S(2)}) copy-start(f32[1536]{0:T(1024)} %get-tuple-element.57) | copy-start | bytes 18436
  129.7 13.4 %copy-start.23 = (f32[1536]{0:T(1024)S(1)}, f32[1536]{0:T(1024)}, u32[]{:S(2)}) copy-start(f32[1536]{0:T(1024)} %get-tuple-element.58) | copy-start | bytes 18436
  129.7 13.4 %copy-start.25 = (f32[1536]{0:T(1024)S(1)}, f32[1536]{0:T(1024)}, u32[]{:S(2)}) copy-start(f32[1536]{0:T(1024)} %get-tuple-element.59) | copy-start | bytes 18436
  129.7 13.4 %copy-start.27 = (f32[1536]{0:T(1024)S(1)}, f32[1536]{0:T(1024)}, u32[]{:S(2)}) copy-start(f32[1536]{0:T(1024)} %get-tuple-element.60) | copy-start | bytes 18436
  129.7 13.4 %copy-start.29 = (f32[1536]{0:T(1024)S(1)}, f32[1536]{0:T(1024)}, u32[]{:S(2)}) copy-start(f32[1536]{0:T(1024)} %get-tuple-element.61) | copy-start | bytes 18436
  129.7 13.4 %copy-start.31 = (f32[1536]{0:T(1024)S(1)}, f32[1536]{0:T(1024)}, u32[]{:S(2)}) copy-start(f32[1536]{0:T(1024)} %get-tuple-element.62) | copy-start | bytes 18436
  129.7 13.4 %copy-start.33 = (f32[1536]{0:T(1024)S(1)}, f32[1536]{0:T(1024)}, u32[]{:S(2)}) copy-start(f32[1536]{0:T(1024)} %get-tuple-element.63) | copy-start | bytes 18436
  129.7 13.4 %copy-start.35 = (f32[1536]{0:T(1024)S(1)}, f32[1536]{0:T(1024)}, u32[]{:S(2)}) copy-start(f32[1536]{0:T(1024)} %get-tuple-element.64) | copy-start | bytes 18436
  129.7 13.4 %copy-start.37 = (f32[1536]{0:T(1024)S(1)}, f32[1536]{0:T(1024)}, u32[]{:S(2)}) copy-start(f32[1536]{0:T(1024)} %get-tuple-element.65) | copy-start | bytes 18436
  129.7 13.4 %copy-start.39 = (f32[1536]{0:T(1024)S(1)}, f32[1536]{0:T(1024)}, u32[]{:S(2)}) copy-start(f32[1536]{0:T(1024)} %get-tuple-element.66) | copy-start | bytes 18436
  129.7 13.4 %copy-start.41 = (f32[1536]{0:T(1024)S(1)}, f32[1536]{0:T(1024)}, u32[]{:S(2)}) copy-start(f32[1536]{0:T(1024)} %get-tuple-element.67) | copy-start | bytes 18436
  129.8 13.4 %copy-start.43 = (f32[1536]{0:T(1024)S(1)}, f32[1536]{0:T(1024)}, u32[]{:S(2)}) copy-start(f32[1536]{0:T(1024)} %get-tuple-element.68) | copy-start | bytes 18436
  129.8 13.4 %copy-start.45 = (f32[1536]{0:T(1024)S(1)}, f32[1536]{0:T(1024)}, u32[]{:S(2)}) copy-start(f32[1536]{0:T(1024)} %get-tuple-element.69) | copy-start | bytes 18436
  129.8 13.4 %copy-start.47 = (f32[1536]{0:T(1024)S(1)}, f32[1536]{0:T(1024)}, u32[]{:S(2)}) copy-start(f32[1536]{0:T(1024)} %get-tuple-element.70) | copy-start | bytes 18436
  129.8 13.4 %copy-start.49 = (f32[1536]{0:T(1024)S(1)}, f32[1536]{0:T(1024)}, u32[]{:S(2)}) copy-start(f32[1536]{0:T(1024)} %copy-done.48) | copy-start | bytes 18436
  129.8 13.4 %copy-start.51 = (f32[1536]{0:T(1024)S(1)}, f32[1536]{0:T(1024)}, u32[]{:S(2)}) copy-start(f32[1536]{0:T(1024)} %copy-done.50) | copy-start | bytes 18436
  129.8 13.4 %copy-start.53 = (f32[1536]{0:T(1024)S(1)}, f32[1536]{0:T(1024)}, u32[]{:S(2)}) copy-start(f32[1536]{0:T(1024)} %copy-done.52) | copy-start | bytes 18436
  129.8 13.4 %copy-start.55 = (f32[1536]{0:T(1024)S(1)}, f32[1536]{0:T(1024)}, u32[]{:S(2)}) copy-start(f32[1536]{0:T(1024)} %copy-done.54) | copy-start | bytes 18436
  129.8 13.4 %copy-start.57 = (f32[1536]{0:T(1024)S(1)}, f32[1536]{0:T(1024)}, u32[]{:S(2)}) copy-start(f32[1536]{0:T(1024)} %copy-done.56) | copy-start | bytes 18436
  129.8 13.4 %copy-start.59 = (f32[1536]{0:T(1024)S(1)}, f32[1536]{0:T(1024)}, u32[]{:S(2)}) copy-start(f32[1536]{0:T(1024)} %copy-done.58) | copy-start | bytes 18436
  129.8 13.4 %copy-start.61 = (f32[1536]{0:T(1024)S(1)}, f32[1536]{0:T(1024)}, u32[]{:S(2)}) copy-start(f32[1536]{0:T(1024)} %copy-done.60) | copy-start | bytes 18436
  129.9 13.4 %copy-start.63 = (f32[1536]{0:T(1024)S(1)}, f32[1536]{0:T(1024)}, u32[]{:S(2)}) copy-start(f32[1536]{0:T(1024)} %copy-done.62) | copy-start | bytes 18436
  129.9 13.4 %copy-start.65 = (f32[1536]{0:T(1024)S(1)}, f32[1536]{0:T(1024)}, u32[]{:S(2)}) copy-start(f32[1536]{0:T(1024)} %copy-done.64) | copy-start | bytes 18436
  129.9 13.4 %copy-start.67 = (f32[1536]{0:T(1024)S(1)}, f32[1536]{0:T(1024)}, u32[]{:S(2)}) copy-start(f32[1536]{0:T(1024)} %copy-done.66) | copy-start | bytes 18436
  129.9 13.4 %copy-start.69 = (f32[1536]{0:T(1024)S(1)}, f32[1536]{0:T(1024)}, u32[]{:S(2)}) copy-start(f32[1536]{0:T(1024)} %copy-done.68) | copy-start | bytes 18436
  137.5 3.4 collective-permute-start.3
  139.6 3.5 collective-permute-start.2
  153.0 132.4 %reduce-scatter.10.cloned.1.call-start = ((), (), s32[]{:S(2)}) async-start(), calls=%async_computation.13 | async-start | bytes 491520
  158.4 210.9 %all-reduce.2.cloned.1.call-start = ((), (), s32[]{:S(2)}) async-start(), calls=%async_computation.11 | async-start | bytes 2359296 | tf_op jit(solution)/shard_map/psum | solution.py:161
  181.3 551.1 %all-gather.9.cloned.1.call-start = ((), (), s32[]{:S(2)}) async-start(), calls=%async_computation.12 | async-start | bytes 21233664 | tf_op jit(solution)/shard_map/all_gather | solution.py:11
  732.4 13.6 %copy-start.1 = (bf16[1,128,1536]{2,1,0:T(8,128)(2,1)S(1)}, bf16[1,128,1536]{2,1,0:T(8,128)(2,1)}, u32[]{:S(2)}) copy-start(bf16[1,128,1536]{2,1,0:T(8,128)(2,1)} %param.19) | copy-start | bytes 1179652
  (53 other events, 372.4 us)
Sparse Core Ops, SparseCore 0:
  9.6 80.9 all-gather.6
  92.1 37.4 all-gather.4
  132.7 48.4 reduce-scatter.7
  183.7 77.8 reduce-scatter.5
  264.5 20.8 reduce-scatter.9
  288.8 80.4 all-reduce.1
  370.8 361.5 all-gather.8
